TPU v7x, 256 devices: a whole 4x4x8 slice. The times are simulated.
256 devices in a mesh: occ: 64 (over x, z, core), aux: 4 (over y).
Axes of the slice: x: 4, y: 4, z: 8, core: 2. Of those that a mesh axis runs over, the one named last changes fastest.
Arguments:
- factors: bfloat16 [128, 256, 1024], P('occ', None, 'aux'), may hold values from -0.8984375 to 0.8984375
- occ_energy: float32 [128], replicated, may hold values from -3 to -0.5
- vir_energy: float32 [256], replicated, may hold values from 0.5 to 3
- i_slot: int32 [2048], P('occ'), may hold values from 0 to 1
- j_slot: int32 [2048], P('occ'), may hold values from 0 to 1
- partner_device: int32 [2048, 1], P('occ'), may hold values from 0 to 63; in each aligned block of 32 rows (0 to 31, 32 to 63, ...) at most 2 rows name the same one
- pair_count: int32 [64], P('occ'), may hold values from 1 to 32, 1843 in all
Outputs:
- gamma: float32 [128, 256, 1024], P('occ', None, 'aux')
- aux_matrix: float32 [1024, 1024], P('aux', 'occ')
Inputs may be any that keep to these rules, and one draw needn't show every extreme that they name: `partner_device`: among the 32 pair slots of one occ index, at most 2 name the same partner device, and some index reaches 2.
All inputs are finite; a program needn't handle non-finite values. No bound on the sum of `pair_count` on one device may be relied on, other than what follows from the above.
Results may differ from a plain program's by a relative error of at most 0.0013.
Values may be sent and summed in bfloat16 or wider, within the bound.
No kernel may reach another device: no remote copies, remote signals or barrier semaphores. Data moves between devices by JAX's collectives and lax.ppermute only.
A program may use at most 128 MiB of HBM per device.

v0:
```python
import jax
import jax.numpy as jnp
from jax import lax
from jax.sharding import PartitionSpec as P


def body(factors, occ_energy, vir_energy, i_slot, j_slot, partner_device, pair_count):
    held, virtuals, columns = factors.shape
    pair_slots = i_slot.shape[0]
    occ_count = lax.axis_size("occ")
    capacity = max(2, (3 * pair_slots // 2 + occ_count - 1) // occ_count)
    slot_total = occ_count * capacity
    device_index = lax.axis_index("occ")
    pair_order = jnp.arange(pair_slots, dtype=jnp.int32)
    living = pair_order < pair_count[0]
    target = partner_device[:, 0]
    earlier = (
        (target[:, None] == target[None, :])
        & living[None, :]
        & (pair_order[None, :] < pair_order[:, None])
    )
    slot_rank = jnp.sum(earlier.astype(jnp.int32), axis=1)
    slot_index = target * capacity + slot_rank
    slot_hit = (slot_index[:, None] == jnp.arange(slot_total, dtype=jnp.int32)[None, :]) & living[
        :, None
    ]
    requests = jnp.sum(jnp.where(slot_hit, j_slot[:, None] + 1, 0), axis=0) - 1
    wanted = lax.all_to_all(requests, "occ", split_axis=0, concat_axis=0, tiled=True)
    wanted_hit = (wanted[:, None] == jnp.arange(held, dtype=jnp.int32)[None, :]).astype(
        jnp.bfloat16
    )
    factor_rows = factors.reshape(held, virtuals * columns)
    far_index = target * held + j_slot
    outgoing = jnp.dot(wanted_hit, factor_rows, preferred_element_type=jnp.float32)
    outgoing = outgoing.astype(jnp.bfloat16).reshape(slot_total, virtuals, columns)
    arrived = lax.all_to_all(outgoing, "occ", split_axis=0, concat_axis=0, tiled=True)
    pick_rows = slot_hit.astype(jnp.bfloat16)
    partner_blocks = jnp.dot(
        pick_rows,
        arrived.reshape(slot_total, virtuals * columns),
        preferred_element_type=jnp.float32,
    )
    partner_blocks = partner_blocks.astype(jnp.bfloat16).reshape(pair_slots, virtuals, columns)
    own_blocks = factors[i_slot]
    orbitals = occ_energy.shape[0]
    table = jnp.arange(orbitals, dtype=jnp.int32)
    own_index = device_index * held + i_slot
    energy_own = jnp.sum(
        jnp.where(own_index[:, None] == table[None, :], occ_energy[None, :], 0.0), axis=1
    )
    energy_far = jnp.sum(
        jnp.where(far_index[:, None] == table[None, :], occ_energy[None, :], 0.0), axis=1
    )
    denominator = (
        vir_energy[None, :, None]
        + vir_energy[None, None, :]
        - energy_own[:, None, None]
        - energy_far[:, None, None]
    )
    partial_value = jnp.einsum(
        "pvq,pwq->pvw", own_blocks, partner_blocks, preferred_element_type=jnp.float32
    )
    summed = lax.psum(partial_value, "aux")
    amplitude = jnp.where(living[:, None, None], summed / denominator, 0.0).astype(jnp.bfloat16)
    local_terms = jnp.einsum(
        "pvw,pwq->pvq", amplitude, partner_blocks, preferred_element_type=jnp.float32
    )
    owner_hit = (i_slot[:, None] == jnp.arange(held, dtype=jnp.int32)[None, :]).astype(jnp.float32)
    gamma_local = jnp.einsum("po,pvq->ovq", owner_hit, local_terms, precision=lax.Precision.HIGHEST)
    return_terms = jnp.einsum(
        "pwv,pwq->pvq", amplitude, own_blocks, preferred_element_type=jnp.float32
    ).astype(jnp.bfloat16)
    placed = jnp.dot(
        slot_hit.astype(jnp.bfloat16).T,
        return_terms.reshape(pair_slots, virtuals * columns),
        preferred_element_type=jnp.float32,
    )
    placed = placed.astype(jnp.bfloat16).reshape(slot_total, virtuals, columns)
    returned = lax.all_to_all(placed, "occ", split_axis=0, concat_axis=0, tiled=True)
    gathered_back = jnp.dot(
        wanted_hit.T,
        returned.reshape(slot_total, virtuals * columns),
        preferred_element_type=jnp.float32,
    )
    gamma = gamma_local + gathered_back.reshape(held, virtuals, columns)
    rounded = gamma.astype(jnp.bfloat16)
    stacked = jnp.stack([rounded, factors])
    gamma_rows = rounded.reshape(held * virtuals, columns)
    factor_flat = factors.reshape(held * virtuals, columns)
    piece = lax.all_gather(stacked, "aux", axis=3, tiled=True)
    width_here = piece.shape[3]
    gamma_piece = piece[0].reshape(held * virtuals, width_here)
    factor_piece = piece[1].reshape(held * virtuals, width_here)
    first = jnp.dot(gamma_rows.T, factor_piece, preferred_element_type=jnp.float32)
    second = jnp.dot(factor_flat.T, gamma_piece, preferred_element_type=jnp.float32)
    terms = first + second
    shared = lax.psum_scatter(terms, "occ", scatter_dimension=1, tiled=True)
    factor_scale = float(orbitals * virtuals) ** (-0.5)
    return (gamma, shared * factor_scale)


def solution(mesh):
    placed = (P("occ", None, "aux"), P(), P(), P("occ"), P("occ"), P("occ", None), P("occ"))
    return jax.shard_map(
        body,
        mesh=mesh,
        in_specs=placed,
        out_specs=(P("occ", None, "aux"), P("aux", "occ")),
        check_vma=False,
    )
```

profile of v0, /device:TPU:8, one launch (start us, length us, event | category | flops | bytes accessed | tf_op | source)
XLA Modules:
  0.0 1268.4 jit_solution(14306813267259421610)
XLA Ops:
  7.8 0.9 convert_reduce_fusion
  11.0 11.9 all-to-all-start
  22.9 1.2 copy.40
  24.1 8.2 all-to-all-done
  33.7 8.1 convolution_convert_fusion.1
  41.8 15.6 %copy.41 = bf16[16,8,256,256]{3,2,1,0:T(8,128)(2,1)} copy(bf16[16,8,256,256]{3,1,2,0:T(8,128)(2,1)} %bitcast.69) | data formatting | bytes 33554432
  57.5 6.0 all-to-all-start.1
  63.8 2.9 gather_fusion
  66.7 361.4 %all-to-all-done.1 = bf16[128,256,256]{2,1,0:T(8,128)(2,1)} async-done(((bf16[128,256,256]{2,1,0:T(8,128)(2,1)}), bf16[128,256,256]{2,1,0:T(8,128)(2,1)}, u32[]{:S(2)}, u32[]{:S(2)}) %all-to-all-start.1) | async-done | bytes 16777248 | tf_op jit(solution)/shard_map/all_to_all | solution.py:36
  428.1 15.8 %copy.42 = bf16[16,8,256,256]{3,1,2,0:T(8,128)(2,1)S(1)} copy(bf16[16,8,256,256]{3,2,1,0:T(8,128)(2,1)} %bitcast.23) | data formatting | bytes 33554432
  443.9 3.9 convolution_convert_fusion.2
  447.8 3.3 copy.43
  451.2 1.9 copy-done.2
  453.1 4.5 fusion.26
  458.6 161.0 %all-reduce.2.cloned.1.call-done = f32[32,256,256]{2,1,0:T(8,128)} async-done(((f32[32,256,256]{2,1,0:T(8,128)}), f32[32,256,256]{2,1,0:T(8,128)}) %all-reduce.2.cloned.1.call-update) | async-done | bytes 8388624 | tf_op jit(solution)/shard_map/psum | solution.py:63
  619.6 5.0 select_convert_fusion
  624.6 1.3 convolution_convert_fusion.3
  625.9 4.4 copy.44
  630.3 12.5 convolution_convert_fusion
  642.9 15.6 %copy.45 = bf16[16,8,256,256]{3,2,1,0:T(8,128)(2,1)} copy(bf16[16,8,256,256]{3,1,2,0:T(8,128)(2,1)} %bitcast.68) | data formatting | bytes 33554432
  658.5 10.7 all-to-all-start.2
  669.5 7.9 fusion.27
  677.4 356.4 %all-to-all-done.2 = bf16[128,256,256]{2,1,0:T(8,128)(2,1)} async-done(((bf16[128,256,256]{2,1,0:T(8,128)(2,1)}), bf16[128,256,256]{2,1,0:T(8,128)(2,1)}, u32[]{:S(2)}, u32[]{:S(2)}) %all-to-all-start.2) | async-done | bytes 16777248 | tf_op jit(solution)/shard_map/all_to_all | solution.py:79
  1033.8 23.4 %copy.39 = bf16[128,256,256]{0,2,1:T(8,128)(2,1)} copy(bf16[128,256,256]{2,1,0:T(8,128)(2,1)} %all-to-all-done.2) | data formatting | bytes 33554432 | tf_op jit(solution)/shard_map/reshape | solution.py:82
  1057.3 10.2 fusion
  1067.5 10.6 fusion.25
  1078.0 1.6 pad_maximum_fusion
  1079.7 33.1 %all-gather.2.cloned.1.call-done = bf16[2,2,256,1024]{3,1,2,0:T(2,128)(2,1)} async-done(((bf16[2,2,256,256]{3,1,2,0:T(2,128)(2,1)}), bf16[2,2,256,1024]{3,1,2,0:T(2,128)(2,1)}) %all-gather.2.cloned.1.call-update) | async-done | bytes 2097168 | tf_op jit(solution)/shard_map/all_gather | solution.py:90
  1112.8 2.9 fusion.24
  1116.8 1.4 fusion.4
  1119.1 141.2 %reduce-scatter.2.cloned.1.call-done = f32[256,16]{0,1:T(8,128)} async-done(((f32[256,1024]{0,1:T(8,128)}), f32[256,16]{0,1:T(8,128)}) %reduce-scatter.2.cloned.1.call-update) | async-done | bytes 16400 | tf_op jit(solution)/shard_map/reduce_scatter | solution.py:97
  1260.3 1.3 broadcast_multiply_fusion
  (39 shorter events, 7.2 us)
Async XLA Ops:
  11.0 21.4 %all-to-all-start = ((s32[64,2,1]{1,2,0:T(1,128)}), s32[64,2,1]{1,2,0:T(1,128)S(1)}, u32[]{:S(2)}, u32[]{:S(2)}) async-start(s32[64,2,1]{1,2,0:T(1,128)} %bitcast.5), calls=%async_computation | async-start | bytes 65536 | tf_op jit(solution)/shard_map/all_to_all | solution.py:28
  57.5 6.4 copy-start
  57.5 370.7 %all-to-all-start.1 = ((bf16[128,256,256]{2,1,0:T(8,128)(2,1)}), bf16[128,256,256]{2,1,0:T(8,128)(2,1)}, u32[]{:S(2)}, u32[]{:S(2)}) async-start(bf16[128,256,256]{2,1,0:T(8,128)(2,1)} %bitcast.66), calls=%async_computation.1 | async-start | bytes 33554432 | tf_op jit(solution)/shard_map/all_to_all | solution.py:36
  63.5 556.1 %all-reduce.2.cloned.1.call-start = ((), (), s32[]{:S(2)}) async-start(), calls=%async_computation.4 | async-start | bytes 16777216 | tf_op jit(solution)/shard_map/psum | solution.py:63
  447.8 5.3 copy-start.3
  451.2 1.9 copy-start.2
  457.6 0.7 copy-start.7
  457.6 0.8 copy-start.5
  619.6 5.0 copy-start.4
  624.6 5.7 copy-start.1
  658.5 375.4 %all-to-all-start.2 = ((bf16[128,256,256]{2,1,0:T(8,128)(2,1)}), bf16[128,256,256]{2,1,0:T(8,128)(2,1)}, u32[]{:S(2)}, u32[]{:S(2)}) async-start(bf16[128,256,256]{2,1,0:T(8,128)(2,1)} %bitcast.67), calls=%async_computation.2 | async-start | bytes 33554432 | tf_op jit(solution)/shard_map/all_to_all | solution.py:79
  669.2 443.6 %all-gather.2.cloned.1.call-start = ((), (), s32[]{:S(2)}) async-start(), calls=%async_computation.5 | async-start | bytes 2621440 | tf_op jit(solution)/shard_map/all_gather | solution.py:90
  1057.3 10.2 copy-start.6
  1079.6 180.7 %reduce-scatter.2.cloned.1.call-start = ((), (), s32[]{:S(2)}) async-start(), calls=%async_computation.6 | async-start | bytes 1064960 | tf_op jit(solution)/shard_map/reduce_scatter | solution.py:97
Sparse Core Ops, SparseCore 0:
  457.8 161.7 all-reduce.1
  1079.7 33.0 all-gather.1
  1118.4 141.9 reduce-scatter.1
where the time goes:
time: 1270 us
  waiting for transfers between devices  1060 us (83%)
  local copies, waits for them, and re-layouts  90.8 us (7%)
  matrix products  61 us (5%)
  starting transfers between devices  29.1 us (2%)
  between operations  14.8 us (1%)
    all_to_all x1, waiting for transfers between devices, body(): lax.all_to_all(outgoing, 'occ', split_axis=0, concat_axis=0, tiled=True)  361 us
    all_to_all x1, waiting for transfers between devices, body(): lax.all_to_all(placed, 'occ', split_axis=0, concat_axis=0, tiled=True)  356 us
    psum x1, waiting for transfers between devices, body(): summed = lax.psum(partial_value, 'aux')  161 us
    reduce_scatter x1, waiting for transfers between devices, body(): shared = lax.psum_scatter(terms, 'occ', scatter_dimension=1, tiled=True)  141 us
    unnamed x24, local copies, waits for them, and re-layouts  59.7 us
    all_gather x1, waiting for transfers between devices, body(): piece = lax.all_gather(stacked, 'aux', axis=3, tiled=True)  33.1 us
  transfers between devices with their start and end apart: 6, of which 6 were waited for; matrix products, arithmetic and copies ran while one was open for 1% of the time, Pallas kernels for 0%

commit v1 on v0

--- a/solution.py
+++ b/solution.py
@@ -60,7 +60,7 @@
     partial_value = jnp.einsum(
         "pvq,pwq->pvw", own_blocks, partner_blocks, preferred_element_type=jnp.float32
     )
-    summed = lax.psum(partial_value, "aux")
+    summed = jnp.sum(lax.all_gather(partial_value, "aux"), axis=0)
     amplitude = jnp.where(living[:, None, None], summed / denominator, 0.0).astype(jnp.bfloat16)
     local_terms = jnp.einsum(
         "pvw,pwq->pvq", amplitude, partner_blocks, preferred_element_type=jnp.float32

time: 1270 us -> 1420 us (1.12)
  waiting for transfers between devices: 1060 us -> 1190 us
  other arithmetic: 11.3 us -> 26.9 us
    all_gather x0 -> x1, waiting for transfers between devices: none -> 293 us  [body(): summed = jnp.sum(lax.all_gather(partial_value, 'aux'), axis=0)]
    psum x1 -> x0, waiting for transfers between devices: 161 us -> none  [body(): summed = lax.psum(partial_value, 'aux')]
    reduce_sum x0 -> x1, other arithmetic: none -> 16 us  [body(): summed = jnp.sum(lax.all_gather(partial_value, 'aux'), axis=0)]
where the time goes in v1:
time: 1420 us
  waiting for transfers between devices  1190 us (84%)
  local copies, waits for them, and re-layouts  90.8 us (6%)
  matrix products  61 us (4%)
  starting transfers between devices  29.3 us (2%)
  other arithmetic  26.9 us (2%)
  between operations  14.9 us (1%)
    all_to_all x1, waiting for transfers between devices, body(): lax.all_to_all(outgoing, 'occ', split_axis=0, concat_axis=0, tiled=True)  361 us
    all_to_all x1, waiting for transfers between devices, body(): lax.all_to_all(placed, 'occ', split_axis=0, concat_axis=0, tiled=True)  356 us
    all_gather x1, waiting for transfers between devices, body(): summed = jnp.sum(lax.all_gather(partial_value, 'aux'), axis=0)  293 us
    reduce_scatter x1, waiting for transfers between devices, body(): shared = lax.psum_scatter(terms, 'occ', scatter_dimension=1, tiled=True)  141 us
    unnamed x24, local copies, waits for them, and re-layouts  59.7 us
    all_gather x1, waiting for transfers between devices, body(): piece = lax.all_gather(stacked, 'aux', axis=3, tiled=True)  33.1 us
  transfers between devices with their start and end apart: 6, of which 6 were waited for; matrix products, arithmetic and copies ran while one was open for 1% of the time, Pallas kernels for 0%

profile of v1, /device:TPU:8, one launch (start us, length us, event | category | flops | bytes accessed | tf_op | source)
XLA Modules:
  0.0 1416.3 jit_solution(14598139161936386033)
XLA Ops:
  11.0 11.9 all-to-all-start
  22.9 1.2 copy.38
  24.1 8.2 all-to-all-done
  33.7 8.1 convolution_convert_fusion.1
  41.8 15.6 %copy.39 = bf16[16,8,256,256]{3,2,1,0:T(8,128)(2,1)} copy(bf16[16,8,256,256]{3,1,2,0:T(8,128)(2,1)} %bitcast.70) | data formatting | bytes 33554432
  57.5 6.0 all-to-all-start.1
  64.1 2.7 gather_fusion
  66.8 361.3 %all-to-all-done.1 = bf16[128,256,256]{2,1,0:T(8,128)(2,1)} async-done(((bf16[128,256,256]{2,1,0:T(8,128)(2,1)}), bf16[128,256,256]{2,1,0:T(8,128)(2,1)}, u32[]{:S(2)}, u32[]{:S(2)}) %all-to-all-start.1) | async-done | bytes 16777248 | tf_op jit(solution)/shard_map/all_to_all | solution.py:36
  428.1 15.8 %copy.40 = bf16[16,8,256,256]{3,1,2,0:T(8,128)(2,1)S(1)} copy(bf16[16,8,256,256]{3,2,1,0:T(8,128)(2,1)} %bitcast.24) | data formatting | bytes 33554432
  443.9 3.9 convolution_convert_fusion.2
  447.8 3.3 copy.41
  451.2 1.9 copy-done.2
  453.1 4.5 fusion.26
  458.6 293.2 %all-gather.6.cloned.1.call-done = f32[128,256,256]{2,1,0:T(8,128)} async-done(((f32[32,256,256]{2,1,0:T(8,128)}), f32[128,256,256]{2,1,0:T(8,128)}) %all-gather.6.cloned.1.call-update) | async-done | bytes 33554448 | tf_op jit(solution)/shard_map/all_gather | solution.py:63
  751.8 16.0 %reduce_sum.50 = f32[32,256,256]{2,1,0:T(8,128)} reduce(f32[4,32,256,256]{3,2,1,0:T(8,128)} %bitcast.74, f32[]{:T(128)} %constant.5.clone.1), dimensions={0}, to_apply=%region_2.3 | reduce | flops 6291456 | bytes 41943044 | tf_op jit(solution)/shard_map/reduce_sum | solution.py:63
  767.8 4.7 select_convert_fusion
  772.5 1.3 convolution_convert_fusion.3
  773.8 4.4 copy.42
  778.2 12.5 convolution_convert_fusion
  790.7 15.6 %copy.43 = bf16[16,8,256,256]{3,2,1,0:T(8,128)(2,1)} copy(bf16[16,8,256,256]{3,1,2,0:T(8,128)(2,1)} %bitcast.69) | data formatting | bytes 33554432
  806.3 10.7 all-to-all-start.2
  817.3 7.9 fusion.27
  825.3 356.4 %all-to-all-done.2 = bf16[128,256,256]{2,1,0:T(8,128)(2,1)} async-done(((bf16[128,256,256]{2,1,0:T(8,128)(2,1)}), bf16[128,256,256]{2,1,0:T(8,128)(2,1)}, u32[]{:S(2)}, u32[]{:S(2)}) %all-to-all-start.2) | async-done | bytes 16777248 | tf_op jit(solution)/shard_map/all_to_all | solution.py:79
  1181.7 23.5 %copy.37 = bf16[128,256,256]{0,2,1:T(8,128)(2,1)} copy(bf16[128,256,256]{2,1,0:T(8,128)(2,1)} %all-to-all-done.2) | data formatting | bytes 33554432 | tf_op jit(solution)/shard_map/reshape | solution.py:82
  1205.2 10.2 fusion
  1215.4 10.6 fusion.25
  1225.9 1.6 pad_maximum_fusion
  1227.6 33.1 %all-gather.4.cloned.1.call-done = bf16[2,2,256,1024]{3,1,2,0:T(2,128)(2,1)} async-done(((bf16[2,2,256,256]{3,1,2,0:T(2,128)(2,1)}), bf16[2,2,256,1024]{3,1,2,0:T(2,128)(2,1)}) %all-gather.4.cloned.1.call-update) | async-done | bytes 2097168 | tf_op jit(solution)/shard_map/all_gather | solution.py:90
  1260.7 2.9 fusion.24
  1264.7 1.4 fusion.4
  1267.0 141.2 %reduce-scatter.2.cloned.1.call-done = f32[256,16]{0,1:T(8,128)} async-done(((f32[256,1024]{0,1:T(8,128)}), f32[256,16]{0,1:T(8,128)}) %reduce-scatter.2.cloned.1.call-update) | async-done | bytes 16400 | tf_op jit(solution)/shard_map/reduce_scatter | solution.py:97
  1408.2 1.3 broadcast_multiply_fusion
  (40 shorter events, 8.4 us)
Async XLA Ops:
  11.0 21.4 %all-to-all-start = ((s32[64,2,1]{1,2,0:T(1,128)}), s32[64,2,1]{1,2,0:T(1,128)S(1)}, u32[]{:S(2)}, u32[]{:S(2)}) async-start(s32[64,2,1]{1,2,0:T(1,128)} %bitcast.5), calls=%async_computation | async-start | bytes 65536 | tf_op jit(solution)/shard_map/all_to_all | solution.py:28
  57.5 6.6 copy-start
  57.5 370.7 %all-to-all-start.1 = ((bf16[128,256,256]{2,1,0:T(8,128)(2,1)}), bf16[128,256,256]{2,1,0:T(8,128)(2,1)}, u32[]{:S(2)}, u32[]{:S(2)}) async-start(bf16[128,256,256]{2,1,0:T(8,128)(2,1)} %bitcast.67), calls=%async_computation.1 | async-start | bytes 33554432 | tf_op jit(solution)/shard_map/all_to_all | solution.py:36
  63.5 688.3 %all-gather.6.cloned.1.call-start = ((), (), s32[]{:S(2)}) async-start(), calls=%async_computation.6 | async-start | bytes 41943040 | tf_op jit(solution)/shard_map/all_gather | solution.py:63
  447.8 5.3 copy-start.3
  451.2 1.9 copy-start.2
  457.6 0.7 copy-start.7
  457.6 0.8 copy-start.5
  767.8 4.7 copy-start.4
  772.4 5.7 copy-start.1
  806.3 375.4 %all-to-all-start.2 = ((bf16[128,256,256]{2,1,0:T(8,128)(2,1)}), bf16[128,256,256]{2,1,0:T(8,128)(2,1)}, u32[]{:S(2)}, u32[]{:S(2)}) async-start(bf16[128,256,256]{2,1,0:T(8,128)(2,1)} %bitcast.68), calls=%async_computation.2 | async-start | bytes 33554432 | tf_op jit(solution)/shard_map/all_to_all | solution.py:79
  817.0 443.7 %all-gather.4.cloned.1.call-start = ((), (), s32[]{:S(2)}) async-start(), calls=%async_computation.4 | async-start | bytes 2621440 | tf_op jit(solution)/shard_map/all_gather | solution.py:90
  1205.2 10.2 copy-start.6
  1227.5 180.7 %reduce-scatter.2.cloned.1.call-start = ((), (), s32[]{:S(2)}) async-start(), calls=%async_computation.5 | async-start | bytes 1064960 | tf_op jit(solution)/shard_map/reduce_scatter | solution.py:97
Sparse Core Ops, SparseCore 0:
  457.8 293.9 all-gather.5
  1227.6 33.0 all-gather.3
  1266.3 141.8 reduce-scatter.1
